TPU v7x, 32 devices: a whole 2x2x4 slice. The times are simulated.
32 devices in a mesh: dp: 32 (over z, y, x, core).
Axes of the slice: x: 2, y: 2, z: 4, core: 2. Of those that a mesh axis runs over, the one named last changes fastest.
Arguments:
- images: bfloat16 [256, 196, 512], P('dp'), may hold values from -6 to 6
- cotangent: bfloat16 [256, 196, 512], P('dp'), may hold values from -6 to 6
- image_counts: int32 [32], P('dp'), may hold values from 1 to 8, as said below
- shift_mask: int32 [4, 49, 49], replicated, may hold values from 0 to 1, as said below
- rel_index: int32 [49, 49], replicated, may hold values from 0 to 168
- step_count: int32 [1], replicated, may hold values from 1 to 20
- attend_weight: bfloat16 [512, 1536], P('dp'), may hold values from -0.25 to 0.25
- merge_weight: bfloat16 [512, 512], P('dp'), may hold values from -1 to 1
- expand_weight: bfloat16 [512, 2048], P('dp'), may hold values from -0.25 to 0.25
- project_weight: bfloat16 [2048, 512], P('dp'), may hold values from -0.125 to 0.125
- norm_gains: float32 [2, 512], replicated, may hold values from 0.1 to 1.9
- norm_shifts: float32 [2, 512], replicated, may hold values from -2 to 2
- layer_biases: float32 [4608], replicated, may hold values from -2 to 2
- bias_table: float32 [169, 16], replicated, may hold values from -4 to 4
- attend_momentum: float32 [512, 1536], P('dp'), may hold values from -1.2 to 1.2
- merge_momentum: float32 [512, 512], P('dp'), may hold values from -1.2 to 1.2
- expand_momentum: float32 [512, 2048], P('dp'), may hold values from -1.2 to 1.2
- project_momentum: float32 [2048, 512], P('dp'), may hold values from -1.2 to 1.2
- gains_mean: float32 [2, 512], replicated, may hold values from -0.6 to 0.6
- gains_square: float32 [2, 512], replicated, may hold values from 0.0001 to 0.001
- shifts_mean: float32 [2, 512], replicated, may hold values from -0.6 to 0.6
- shifts_square: float32 [2, 512], replicated, may hold values from 0.0001 to 0.001
- biases_mean: float32 [4608], replicated, may hold values from -0.6 to 0.6
- biases_square: float32 [4608], replicated, may hold values from 0.0001 to 0.001
- table_mean: float32 [169, 16], replicated, may hold values from -0.6 to 0.6
- table_square: float32 [169, 16], replicated, may hold values from 0.0001 to 0.001
Outputs:
- block_out: bfloat16 [256, 196, 512], P('dp')
- input_grad: float32 [256, 196, 512], P('dp')
- attend_grad: float32 [512, 1536], P('dp')
- attend_momentum_next: float32 [512, 1536], P('dp')
- attend_update: float32 [512, 1536], P('dp')
- merge_grad: float32 [512, 512], P('dp')
- merge_momentum_next: float32 [512, 512], P('dp')
- merge_update: float32 [512, 512], P('dp')
- expand_grad: float32 [512, 2048], P('dp')
- expand_momentum_next: float32 [512, 2048], P('dp')
- expand_update: float32 [512, 2048], P('dp')
- project_grad: float32 [2048, 512], P('dp')
- project_momentum_next: float32 [2048, 512], P('dp')
- project_update: float32 [2048, 512], P('dp')
- gains_grad: float32 [2, 512], replicated
- gains_mean_next: float32 [2, 512], replicated
- gains_square_next: float32 [2, 512], replicated
- gains_update: float32 [2, 512], replicated
- shifts_grad: float32 [2, 512], replicated
- shifts_mean_next: float32 [2, 512], replicated
- shifts_square_next: float32 [2, 512], replicated
- shifts_update: float32 [2, 512], replicated
- biases_grad: float32 [4608], replicated
- biases_mean_next: float32 [4608], replicated
- biases_square_next: float32 [4608], replicated
- biases_update: float32 [4608], replicated
- table_grad: float32 [169, 16], replicated
- table_mean_next: float32 [169, 16], replicated
- table_square_next: float32 [169, 16], replicated
- table_update: float32 [169, 16], replicated
Inputs may be any that keep to these rules, and one draw needn't show every extreme that they name: `image_counts`: one device holds 8 live images and another holds 1; live images fill a device's first slots. `shift_mask`: 1 where two patches of a window may attend to each other; symmetric, with ones on the diagonal.
All inputs are finite; a program needn't handle non-finite values.
Results may differ from a plain program's by a relative error of at most 0.0095.
The roundings to bfloat16 on the way count: a program that leaves them out, or rounds other values in their place, can miss the bound.
Values may be sent and summed in bfloat16 or wider, within the bound.
No kernel may reach another device: no remote copies, remote signals or barrier semaphores. Data moves between devices by JAX's collectives and lax.ppermute only.
A program may use at most 256 MiB of HBM per device.

v0:
```python
from functools import partial
import math
import jax
import jax.numpy as jnp
from jax import lax
from jax.sharding import PartitionSpec as P

HEADS = 16
WIN = 7
SIDE = 14
SHIFT = 3
WIN_TOK = 49
PATCHES = 196
TABLE = 169
highest = lax.Precision.HIGHEST
newton_first = 3.4445
newton_second = -4.775
newton_third = 2.0315


def as_sent(shard):

    def short(part):
        return part.astype(jnp.bfloat16) if part.dtype == jnp.float32 else part

    return jax.tree.map(short, shard)


def layer_norm(values, gain, shift):
    center = values - jnp.mean(values, axis=-1, keepdims=True)
    spread = jnp.mean(center * center, axis=-1, keepdims=True)
    return center * lax.rsqrt(spread + 1e-05) * gain + shift


def gelu_exact(values):
    return jax.nn.gelu(values, approximate=False)


def to_windows(field):
    count = field.shape[0]
    blocks = SIDE // WIN
    square = field.reshape(count, SIDE, SIDE, field.shape[-1])
    rolled = jnp.roll(square, (-SHIFT, -SHIFT), (1, 2))
    parted = rolled.reshape(count, blocks, WIN, blocks, WIN, field.shape[-1])
    return parted.transpose(0, 1, 3, 2, 4, 5).reshape(
        count * blocks * blocks, WIN * WIN, field.shape[-1]
    )


def from_windows(windows, count):
    blocks = SIDE // WIN
    parted = windows.reshape(count, blocks, blocks, WIN, WIN, windows.shape[-1])
    square = parted.transpose(0, 1, 3, 2, 4, 5).reshape(count, SIDE, SIDE, windows.shape[-1])
    return jnp.roll(square, (SHIFT, SHIFT), (1, 2)).reshape(count, SIDE * SIDE, windows.shape[-1])


def split_heads(rows):
    return rows.reshape(rows.shape[0], rows.shape[1], HEADS, -1).transpose(0, 2, 1, 3)


def merge_heads(rows):
    return rows.transpose(0, 2, 1, 3).reshape(rows.shape[0], rows.shape[2], -1)


def orthogonalize(matrix):
    tall = matrix.shape[0] > matrix.shape[1]
    current = matrix.T if tall else matrix
    current = current / (jnp.sqrt(jnp.sum(current * current)) + 1e-07)
    for sweep in range(5):
        square = jnp.dot(current, current.T, precision=highest)
        mixer = newton_second * square + newton_third * jnp.dot(square, square, precision=highest)
        current = newton_first * current + jnp.dot(mixer, current, precision=highest)
    return current.T if tall else current


def adamw_step(param, grad, first, second, steps):
    first_next = 0.9 * first + 0.1 * grad
    second_next = 0.999 * second + 0.001 * grad * grad
    first_hat = first_next / (1.0 - jnp.power(0.9, steps))
    second_hat = second_next / (1.0 - jnp.power(0.999, steps))
    update = -0.05 * (first_hat / (jnp.sqrt(second_hat) + 1e-08) + 0.05 * param)
    return (first_next, second_next, update)


def padded_rows(flat, length):
    return jnp.pad(flat, ((0, 0), (0, length - flat.shape[1])))


def local(
    images,
    cotangent,
    image_counts,
    shift_mask,
    rel_index,
    step_count,
    attend_weight,
    merge_weight,
    expand_weight,
    project_weight,
    norm_gains,
    norm_shifts,
    layer_biases,
    bias_table,
    attend_momentum,
    merge_momentum,
    expand_momentum,
    project_momentum,
    gains_mean,
    gains_square,
    shifts_mean,
    shifts_square,
    biases_mean,
    biases_square,
    table_mean,
    table_square,
):
    f32 = jnp.float32
    bf16 = jnp.bfloat16
    slots = images.shape[0]
    width = images.shape[2]
    devices = lax.axis_size("dp")
    hidden_units = expand_weight.shape[1]
    scale = 1.0 / math.sqrt(width // HEADS)
    grad_scale = 1.0 / math.sqrt(slots * devices * PATCHES)
    gathered = (
        lax.all_gather(attend_weight, "dp", axis=0, tiled=True),
        lax.all_gather(merge_weight, "dp", axis=0, tiled=True),
        lax.all_gather(expand_weight, "dp", axis=0, tiled=True),
        lax.all_gather(project_weight, "dp", axis=0, tiled=True),
    )
    attend_full, merge_full, expand_full, project_full = gathered
    valid = (jnp.arange(slots) < image_counts[0]).astype(f32)[:, None, None]
    mask_add = -100.0 * (1 - shift_mask).astype(f32)
    masking = jnp.tile(mask_add, (slots, 1, 1))[:, None]
    one_hot = (rel_index.reshape(-1)[:, None] == jnp.arange(TABLE)[None, :]).astype(f32)
    position = jnp.dot(one_hot, bias_table, precision=highest).T.reshape(HEADS, WIN_TOK, WIN_TOK)
    features = images.astype(f32)
    normed, norm_pull = jax.vjp(layer_norm, features, norm_gains[0], norm_shifts[0])
    windows = to_windows(normed.astype(bf16))
    triple = (
        jnp.einsum("wtd,de->wte", windows, attend_full, preferred_element_type=f32)
        + layer_biases[: 3 * width]
    )
    queries = split_heads(triple[..., :width] * scale).astype(bf16)
    keys_low = split_heads(triple[..., width : 2 * width]).astype(bf16)
    values_low = split_heads(triple[..., 2 * width :]).astype(bf16)
    scores = (
        jnp.einsum("whqc,whkc->whqk", queries, keys_low, preferred_element_type=f32)
        + position
        + masking
    )
    attention = jax.nn.softmax(scores, axis=-1)
    attention_low = attention.astype(bf16)
    mixed = merge_heads(
        jnp.einsum("whqk,whkc->whqc", attention_low, values_low, preferred_element_type=f32)
    ).astype(bf16)
    branch = (
        jnp.einsum("wtd,de->wte", mixed, merge_full, preferred_element_type=f32)
        + layer_biases[3 * width : 4 * width]
    )
    middle = features + from_windows(branch, slots)
    normed_two, norm_two_pull = jax.vjp(layer_norm, middle, norm_gains[1], norm_shifts[1])
    normed_low = normed_two.astype(bf16)
    pre_act = (
        jnp.einsum("itd,df->itf", normed_low, expand_full, preferred_element_type=f32)
        + layer_biases[4 * width : 4 * width + hidden_units]
    )
    activated, gelu_pull = jax.vjp(gelu_exact, pre_act)
    active_low = activated.astype(bf16)
    mlp_out = (
        jnp.einsum("itf,fd->itd", active_low, project_full, preferred_element_type=f32)
        + layer_biases[4 * width + hidden_units :]
    )
    block_out = (valid * (middle + mlp_out)).astype(bf16)
    attend_back, merge_back, expand_back, project_back = (
        lax.all_gather(attend_weight, "dp", axis=0, tiled=True),
        lax.all_gather(merge_weight, "dp", axis=0, tiled=True),
        lax.all_gather(expand_weight, "dp", axis=0, tiled=True),
        lax.all_gather(project_weight, "dp", axis=0, tiled=True),
    )
    grad_out = valid * cotangent.astype(f32)
    grad_out_low = grad_out.astype(bf16)
    project_term = jnp.einsum("itf,itd->fd", active_low, grad_out_low, preferred_element_type=f32)
    grad_act = jnp.einsum("itd,fd->itf", grad_out_low, project_back, preferred_element_type=f32)
    grad_pre = gelu_pull(grad_act)[0].astype(bf16)
    expand_term = jnp.einsum("itd,itf->df", normed_low, grad_pre, preferred_element_type=f32)
    grad_normed_two = jnp.einsum("itf,df->itd", grad_pre, expand_back, preferred_element_type=f32)
    grad_mid_norm, gain_two, shift_two = norm_two_pull(grad_normed_two)
    grad_middle = grad_out + grad_mid_norm
    grad_branch = to_windows(grad_middle).astype(bf16)
    merge_term = jnp.einsum("wtd,wte->de", mixed, grad_branch, preferred_element_type=f32)
    grad_mixed = split_heads(
        jnp.einsum("wte,de->wtd", grad_branch, merge_back, preferred_element_type=f32).astype(bf16)
    )
    grad_values = jnp.einsum(
        "whqk,whqc->whkc", attention_low, grad_mixed, preferred_element_type=f32
    )
    grad_attention = jnp.einsum(
        "whqc,whkc->whqk", grad_mixed, values_low, preferred_element_type=f32
    )
    grad_scores = (
        attention * (grad_attention - jnp.sum(grad_attention * attention, axis=-1, keepdims=True))
    ).astype(bf16)
    position_grad = jnp.sum(grad_scores, axis=0, dtype=f32).reshape(HEADS, WIN_TOK * WIN_TOK)
    table_term = jnp.dot(one_hot.T, position_grad.T, precision=highest)
    grad_queries = jnp.einsum("whqk,whkc->whqc", grad_scores, keys_low, preferred_element_type=f32)
    grad_keys = jnp.einsum("whqk,whqc->whkc", grad_scores, queries, preferred_element_type=f32)
    grad_triple = jnp.concatenate(
        [merge_heads(grad_queries) * scale, merge_heads(grad_keys), merge_heads(grad_values)],
        axis=-1,
    ).astype(bf16)
    attend_term = jnp.einsum("wtd,wte->de", windows, grad_triple, preferred_element_type=f32)
    grad_normed = from_windows(
        jnp.einsum("wte,de->wtd", grad_triple, attend_back, preferred_element_type=f32), slots
    )
    grad_feat, gain_one, shift_one = norm_pull(grad_normed)
    input_grad = grad_middle + grad_feat
    bias_term = jnp.concatenate(
        [
            jnp.sum(grad_triple, axis=(0, 1), dtype=f32),
            jnp.sum(grad_branch, axis=(0, 1), dtype=f32),
            jnp.sum(grad_pre, axis=(0, 1), dtype=f32),
            jnp.sum(grad_out_low, axis=(0, 1), dtype=f32),
        ]
    )
    mat_sums = (
        lax.psum_scatter(attend_term, "dp", scatter_dimension=0, tiled=True),
        lax.psum_scatter(merge_term, "dp", scatter_dimension=0, tiled=True),
        lax.psum_scatter(expand_term, "dp", scatter_dimension=0, tiled=True),
        lax.psum_scatter(project_term, "dp", scatter_dimension=0, tiled=True),
    )
    small_sums = lax.psum(
        (jnp.stack([gain_one, gain_two]), jnp.stack([shift_one, shift_two]), bias_term, table_term),
        "dp",
    )
    mat_grads = tuple((term * grad_scale for term in mat_sums))
    small_grads = tuple((term * grad_scale for term in small_sums))
    momenta = (attend_momentum, merge_momentum, expand_momentum, project_momentum)
    momenta_next = tuple((0.95 * moment + grad for moment, grad in zip(momenta, mat_grads)))
    stride = 1
    owner_ranks = [order * stride for order in range(4)]
    rank_index = lax.axis_index("dp")
    shard_sizes = [moment.size for moment in momenta_next]
    longest = max(shard_sizes)
    whole = lax.all_gather(momenta_next, "dp", axis=0, tiled=True)
    owner_terms = tuple(
        (
            lax.cond(
                rank_index == owner_ranks[order],
                partial(orthogonalize, matrix),
                partial(jnp.zeros_like, matrix),
            )
            for order, matrix in enumerate(whole)
        )
    )
    packed = jnp.zeros((devices, longest), f32)
    for order, term in enumerate(owner_terms):
        packed = packed + padded_rows(term.reshape(devices, shard_sizes[order]), longest)
    received = lax.all_to_all(
        as_sent(packed), "dp", split_axis=0, concat_axis=0, tiled=True
    ).astype(packed.dtype)
    orth_rows = tuple(
        (
            received[owner_ranks[order], : shard_sizes[order]].reshape(moment.shape)
            for order, moment in enumerate(momenta_next)
        )
    )
    results = [block_out, input_grad]
    for grad, moment_next, orth_part, matrix in zip(mat_grads, momenta_next, orth_rows, whole):
        update = -0.02 * math.sqrt(max(matrix.shape)) * orth_part
        results += [grad, moment_next, update]
    steps = step_count[0].astype(f32)
    params = (norm_gains, norm_shifts, layer_biases, bias_table)
    states = (
        (gains_mean, gains_square),
        (shifts_mean, shifts_square),
        (biases_mean, biases_square),
        (table_mean, table_square),
    )
    for param, grad, state in zip(params, small_grads, states):
        first_next, second_next, update = adamw_step(param, grad, state[0], state[1], steps)
        results += [grad, first_next, second_next, update]
    return tuple(results)


def solution(mesh):
    return jax.shard_map(
        local,
        mesh=mesh,
        in_specs=(
            P("dp", None, None),
            P("dp", None, None),
            P("dp"),
            P(),
            P(),
            P(),
            P("dp", None),
            P("dp", None),
            P("dp", None),
            P("dp", None),
            P(),
            P(),
            P(),
            P(),
            P("dp", None),
            P("dp", None),
            P("dp", None),
            P("dp", None),
            P(),
            P(),
            P(),
            P(),
            P(),
            P(),
            P(),
            P(),
        ),
        out_specs=(
            P("dp", None, None),
            P("dp", None, None),
            P("dp", None),
            P("dp", None),
            P("dp", None),
            P("dp", None),
            P("dp", None),
            P("dp", None),
            P("dp", None),
            P("dp", None),
            P("dp", None),
            P("dp", None),
            P("dp", None),
            P("dp", None),
            P(),
            P(),
            P(),
            P(),
            P(),
            P(),
            P(),
            P(),
            P(),
            P(),
            P(),
            P(),
            P(),
            P(),
            P(),
            P(),
        ),
        check_vma=False,
    )
```

profile of v0, /device:TPU:0, one launch (start us, length us, event | category | flops | bytes accessed | tf_op | source)
XLA Modules:
  0.0 1322.4 jit_solution(11692982071132868505)
XLA Ops:
  25.4 47.8 %all_gather.41 = bf16[512,512]{1,0:T(8,128)(2,1)} all-gather(bf16[16,512]{1,0:T(8,128)(2,1)S(1)} %copy-done.51), channel_id=1, replica_groups=mesh['dp'=32] {'dp'}, dimensions={0}, use_global_device_ids=true | all-gather | bytes 540672 | tf_op jit(solution)/shard_map/all_gather | solution.py:127
  74.3 6.6 fusion.124
  81.4 3.6 copy.261
  87.4 3.7 copy.260
  91.1 3.6 copy.262
  94.8 11.8 fusion.125
  106.6 7.8 fusion.76
  119.5 5.1 reshape.297
  124.6 4.6 copy.305
  136.4 9.4 fusion.68
  145.8 4.6 copy-done.10
  150.3 31.3 %multiply_convert_fusion.1 = (bf16[8,196,2048]{2,1,0:T(8,128)(2,1)}, f32[8,196,2048]{2,1,0:T(8,128)}) fusion(f32[8,196,2048]{2,1,0:T(8,128)S(1)} %get-tuple-element.268, f32[2048]{0:T(1024)S(1)} %copy-done.46, u8[196,2048]{1,0:T(8,128)(4,1)S(1)} %get-tuple-element.201, u8[196,2048]{1,0:T(8,128)(4,1)S(1)} %get-tuple-element.200), kind=kLoop, calls=%fused_computation.103 | loop fusion | flops 227999744 | bytes 32923648 | tf_op jit(solution)/shard_map/convert_element_type | solution.py:169
  181.7 4.1 all-gather.12.cloned.1.call-done
  185.8 18.7 %convert_reduce_fusion.1 = (f32[2048]{0:T(1024)}, bf16[8,196,2048]{2,1,0:T(8,128)(2,1)}) fusion(f32[8,196,2048]{2,1,0:T(8,128)} %get-tuple-element.249, bf16[2048,512]{1,0:T(8,128)(2,1)} %all-gather.12.cloned.1.call-done, f32[8]{0:T(128)} %compare_convert_fusion, bf16[8,196,512]{2,0,1:T(8,128)(2,1)} %param.35, f32[8,196,2048]{2,1,0:T(8,128)} %copy-done.10, ...), kind=kOutput, calls=%fused_computation.101 | convolution fusion | flops 3345332224 | bytes 35831840 | tf_op jit(solution)/shard_map/itd,fd->itf/dot_general | solution.py:184
  204.5 6.8 fusion.114
  222.8 3.8 reshape.298
  231.0 8.1 reshape.282
  239.1 10.5 copy.230
  249.6 13.1 multiply_reduce_fusion.4
  262.7 14.6 %convert_reduce_fusion = (f32[16,49,49]{1,2,0:T(8,128)}, bf16[32,16,49,49]{2,3,1,0:T(8,128)(2,1)}) fusion(f32[32,16,49,49]{2,3,1,0:T(8,128)} %get-tuple-element.271, f32[32,16,49]{2,1,0:T(8,128)S(1)} %get-tuple-element.270, f32[32,16,49,49]{2,3,1,0:T(8,128)} %get-tuple-element.267, f32[32,16,49]{2,1,0:T(8,128)S(1)} %get-tuple-element.266), kind=kLoop, calls=%fused_computation.90 | loop fusion | flops 7337456 | bytes 12647488 | tf_op jit(solution)/shard_map/reduce_sum | solution.py:204
  277.3 8.5 multiply_convert_fusion.2
  285.8 10.3 convolution_convert_fusion
  296.1 8.8 fusion.79
  307.2 4.9 copy.235
  312.1 4.9 copy.236
  317.0 4.9 copy.237
  322.0 4.9 convert_reduce_fusion.2
  329.3 5.2 fusion.69
  334.6 9.1 convolution_bitcast_fusion.2
  345.1 9.3 convolution_bitcast_fusion.1
  354.6 101.1 %reduce-scatter.7.cloned.1.call-done = f32[16,512]{1,0:T(8,128)} async-done(((f32[512,512]{1,0:T(8,128)}), f32[16,512]{1,0:T(8,128)}) %reduce-scatter.7.cloned.1.call-update) | async-done | bytes 32784 | tf_op jit(solution)/shard_map/reduce_scatter | solution.py:228
  457.2 102.7 %reduce-scatter.5.cloned.1.call-done = f32[16,1536]{1,0:T(8,128)} async-done(((f32[512,1536]{1,0:T(8,128)}), f32[16,1536]{1,0:T(8,128)}) %reduce-scatter.5.cloned.1.call-update) | async-done | bytes 98320 | tf_op jit(solution)/shard_map/reduce_scatter | solution.py:227
  561.6 140.6 %reduce-scatter.9.cloned.1.call-done = f32[16,2048]{1,0:T(8,128)} async-done(((f32[512,2048]{1,0:T(8,128)}), f32[16,2048]{1,0:T(8,128)}) %reduce-scatter.9.cloned.1.call-update) | async-done | bytes 131088 | tf_op jit(solution)/shard_map/reduce_scatter | solution.py:229
  704.3 137.2 %reduce-scatter.11.cloned.1.call-done = f32[64,512]{1,0:T(8,128)} async-done(((f32[2048,512]{1,0:T(8,128)}), f32[64,512]{1,0:T(8,128)}) %reduce-scatter.11.cloned.1.call-update) | async-done | bytes 131088 | tf_op jit(solution)/shard_map/reduce_scatter | solution.py:230
  844.0 7.0 fusion.51
  850.9 3.8 reshape.285
  863.6 31.3 %all-gather.16.cloned.1.call-done = f32[512,512]{1,0:T(8,128)} async-done(((f32[16,512]{1,0:T(8,128)}), f32[512,512]{1,0:T(8,128)}) %all-gather.16.cloned.1.call-update) | async-done | bytes 1048592 | tf_op jit(solution)/shard_map/all_gather | solution.py:245
  895.0 11.3 conditional.5
  906.3 50.5 %all-gather.14.cloned.1.call-done = f32[512,1536]{1,0:T(8,128)} async-done(((f32[16,1536]{1,0:T(8,128)}), f32[512,1536]{1,0:T(8,128)}) %all-gather.14.cloned.1.call-update) | async-done | bytes 3145744 | tf_op jit(solution)/shard_map/all_gather | solution.py:245
  956.8 77.7 %conditional.4 = (f32[32,32768]{1,0:T(8,128)}) conditional(s32[]{:T(128)} %convert_element_type.166, () %tuple.40, f32[512,1536]{1,0:T(8,128)} %all-gather.14.cloned.1.call-done), branch_computations={%region_12.13_spmd, %region_13.15_spmd} | conditional | flops 56387174400 | bytes 97517640 | solution.py:248
  960.8 8.3 fusion.5
  971.0 5.5 convolution_add_fusion.4
  976.5 5.4 fusion.126
  983.9 5.5 convolution_add_fusion.3
  989.4 5.4 fusion.127
  996.7 5.5 convolution_add_fusion.2
  1002.3 5.6 fusion.128
  1009.8 5.5 convolution_add_fusion.1
  1015.3 5.4 fusion.129
  1022.7 5.4 convolution_add_fusion
  1030.0 4.2 pad.16
  1034.5 12.3 conditional.6
  1046.8 39.0 %all-gather.20.cloned.1.call-done = f32[2048,512]{1,0:T(8,128)} async-done(((f32[64,512]{1,0:T(8,128)}), f32[2048,512]{1,0:T(8,128)}) %all-gather.20.cloned.1.call-update) | async-done | bytes 4194320 | tf_op jit(solution)/shard_map/all_gather | solution.py:245
  1085.8 8.3 conditional.7
  1094.1 6.6 fusion.84
  1104.1 4.6 reshape.321
  1108.7 106.6 %all-to-all-start = ((bf16[32,2,16384]{2,1,0:T(2,128)(2,1)}), bf16[32,2,16384]{2,1,0:T(2,128)(2,1)}, u32[]{:S(2)}, u32[]{:S(2)}) async-start(bf16[32,2,16384]{2,1,0:T(2,128)(2,1)} %reshape.321), calls=%async_computation.4 | async-start | bytes 4194304 | tf_op jit(solution)/shard_map/all_to_all | solution.py:259
  1215.4 4.7 fusion.65
  1220.2 3.7 fusion.63
  1224.0 3.6 add_add_fusion.4
  1231.5 3.8 multiply_convert_fusion.3
  1238.1 46.8 %all-reduce.4 = (f32[2,512]{1,0:T(2,128)S(1)}, f32[2,512]{1,0:T(2,128)S(1)}, f32[4608]{0:T(1024)S(1)}, f32[169,16]{0,1:T(8,128)S(1)}) all-reduce(f32[2,512]{1,0:T(2,128)S(1)} %pad_maximum_fusion.9, f32[2,512]{1,0:T(2,128)S(1)} %pad_maximum_fusion.10, f32[4608]{0:T(1024)S(1)} %pad_maximum_fusion.8, ...), channel_id=1, replica_groups=mesh['dp'=32] {'dp'}, use_global_device_ids=true, to_apply=%region_29.30 | all-reduce | flops 9360 | bytes 74880 | tf_op jit(solution)/shard_map/psum | solution.py:232
  1286.9 10.5 reshape.322
  1297.4 11.1 convert_element_type.171
  (278 shorter events, 112.2 us)
Async XLA Ops:
  7.2 9.7 copy-start.2
  7.2 67.1 %all-gather.8.cloned.1.call-start = ((), (), s32[]{:S(2)}) async-start(), calls=%async_computation.5 | async-start | bytes 1622016 | tf_op jit(solution)/shard_map/all_gather | solution.py:126
  7.9 128.4 %all-gather.10.cloned.1.call-start = ((), (), s32[]{:S(2)}) async-start(), calls=%async_computation.6 | async-start | bytes 2162688 | tf_op jit(solution)/shard_map/all_gather | solution.py:128
  8.7 177.1 %all-gather.12.cloned.1.call-start = ((), (), s32[]{:S(2)}) async-start(), calls=%async_computation.7 | async-start | bytes 2162688 | tf_op jit(solution)/shard_map/all_gather | solution.py:129
  9.4 446.3 %reduce-scatter.7.cloned.1.call-start = ((), (), s32[]{:S(2)}) async-start(), calls=%async_computation.10 | async-start | bytes 1081344 | tf_op jit(solution)/shard_map/reduce_scatter | solution.py:228
  11.8 6.9 copy-start.25
  20.3 54.0 %slice-start.2 = ((f32[4608]{0:T(1024)}), f32[1536]{0:T(1024)S(1)}, s32[]{:S(2)}) async-start(f32[4608]{0:T(1024)} %param.46), calls=%async_computation.18 | async-start | bytes 16384 | tf_op jit(solution)/shard_map/slice | solution.py:142
  22.6 58.3 %copy-start.19 = (bf16[32,49,512]{2,0,1:T(8,128)(2,1)}, bf16[32,49,512]{2,0,1:T(8,128)(2,1)S(1)}, u32[]{:S(2)}) copy-start(bf16[32,49,512]{2,0,1:T(8,128)(2,1)S(1)} %reshape.277) | copy-start | bytes 4816900
  106.6 9.8 copy-start.17
  106.6 9.8 copy-start.64
  134.7 199.9 %copy-start = (f32[8,196,512]{2,1,0:T(8,128)}, f32[8,196,512]{2,1,0:T(8,128)S(1)}, u32[]{:S(2)}) copy-start(f32[8,196,512]{2,1,0:T(8,128)S(1)} %get-tuple-element.251) | copy-start | bytes 9633796
  136.4 14.0 %copy-start.46 = (f32[2048]{0:T(1024)S(1)}, f32[2048]{0:T(1024)}, u32[]{:S(2)}) copy-start(f32[2048]{0:T(1024)} %slice.126) | copy-start | bytes 24580
  185.8 18.7 %copy-start.42 = (f32[1,512]{1,0:T(1,128)S(1)}, f32[1,512]{1,0:T(1,128)}, u32[]{:S(2)}) copy-start(f32[1,512]{1,0:T(1,128)} %get-tuple-element.260) | copy-start | bytes 6148
  185.8 18.7 %copy-start.77 = (bf16[512,2048]{1,0:T(8,128)(2,1)S(1)}, bf16[512,2048]{1,0:T(8,128)(2,1)}, u32[]{:S(2)}) copy-start(bf16[512,2048]{1,0:T(8,128)(2,1)} %all-gather.10.cloned.1.call-done) | copy-start | bytes 6291460
  204.5 6.8 copy-start.39
  285.8 10.3 copy-start.15
  296.1 8.8 copy-start.13
  296.1 8.8 copy-start.18
  321.9 238.0 %reduce-scatter.5.cloned.1.call-start = ((), (), s32[]{:S(2)}) async-start(), calls=%async_computation.8 | async-start | bytes 3244032 | tf_op jit(solution)/shard_map/reduce_scatter | solution.py:227
  321.9 7.3 copy-start.20
  334.5 367.7 %reduce-scatter.9.cloned.1.call-start = ((), (), s32[]{:S(2)}) async-start(), calls=%async_computation.12 | async-start | bytes 4325376 | tf_op jit(solution)/shard_map/reduce_scatter | solution.py:229
  343.7 497.8 %reduce-scatter.11.cloned.1.call-start = ((), (), s32[]{:S(2)}) async-start(), calls=%async_computation.14 | async-start | bytes 4325376 | tf_op jit(solution)/shard_map/reduce_scatter | solution.py:230
  354.5 101.2 %copy-start.45 = (f32[16,512]{1,0:T(8,128)S(1)}, f32[16,512]{1,0:T(8,128)}, u32[]{:S(2)}) copy-start(f32[16,512]{1,0:T(8,128)} %param.49) | copy-start | bytes 98308
  354.5 205.5 %copy-start.33 = (f32[16,1536]{1,0:T(8,128)S(1)}, f32[16,1536]{1,0:T(8,128)}, u32[]{:S(2)}) copy-start(f32[16,1536]{1,0:T(8,128)} %param.48) | copy-start | bytes 294916
  354.5 347.7 %copy-start.30 = (f32[16,2048]{1,0:T(8,128)S(1)}, f32[16,2048]{1,0:T(8,128)}, u32[]{:S(2)}) copy-start(f32[16,2048]{1,0:T(8,128)} %param.50) | copy-start | bytes 393220
  354.5 487.1 %copy-start.31 = (f32[64,512]{1,0:T(8,128)S(1)}, f32[64,512]{1,0:T(8,128)}, u32[]{:S(2)}) copy-start(f32[64,512]{1,0:T(8,128)} %param.51) | copy-start | bytes 393220
  354.5 489.5 %copy-start.78 = (bf16[512,1536]{1,0:T(8,128)(2,1)S(1)}, bf16[512,1536]{1,0:T(8,128)(2,1)}, u32[]{:S(2)}) copy-start(bf16[512,1536]{1,0:T(8,128)(2,1)} %all-gather.8.cloned.1.call-done) | copy-start | bytes 4718596
  354.5 540.5 %all-gather.16.cloned.1.call-start = ((), (), s32[]{:S(2)}) async-start(), calls=%async_computation.11 | async-start | bytes 1081344 | tf_op jit(solution)/shard_map/all_gather | solution.py:245
  457.1 499.6 %all-gather.14.cloned.1.call-start = ((), (), s32[]{:S(2)}) async-start(), calls=%async_computation.9 | async-start | bytes 3244032 | tf_op jit(solution)/shard_map/all_gather | solution.py:245
  561.5 472.9 %all-gather.18.cloned.1.call-start = ((), (), s32[]{:S(2)}) async-start(), calls=%async_computation.13 | async-start | bytes 4325376 | tf_op jit(solution)/shard_map/all_gather | solution.py:245
  703.8 382.0 %all-gather.20.cloned.1.call-start = ((), (), s32[]{:S(2)}) async-start(), calls=%async_computation.15 | async-start | bytes 4325376 | tf_op jit(solution)/shard_map/all_gather | solution.py:245
  960.7 10.2 copy-start.16
  1104.1 111.3 %copy-start.4 = (bf16[8,196,512]{2,0,1:T(8,128)(2,1)S(1)}, bf16[8,196,512]{2,0,1:T(8,128)(2,1)}, u32[]{:S(2)}) copy-start(bf16[8,196,512]{2,0,1:T(8,128)(2,1)} %param.34) | copy-start | bytes 4816900
  1104.1 111.3 %copy-start.26 = (f32[8,196]{1,0:T(8,128)S(1)}, f32[8,196]{1,0:T(8,128)}, u32[]{:S(2)}) copy-start(f32[8,196]{1,0:T(8,128)} %copy-done.25) | copy-start | bytes 18820
  1104.1 111.3 %copy-start.41 = (f32[1,512]{1,0:T(1,128)S(1)}, f32[1,512]{1,0:T(1,128)}, u32[]{:S(2)}) copy-start(f32[1,512]{1,0:T(1,128)} %copy-done.40) | copy-start | bytes 6148
  1108.7 111.4 %copy-start.37 = (f32[8,196]{1,0:T(8,128)S(1)}, f32[8,196]{1,0:T(8,128)}, u32[]{:S(2)}) copy-start(f32[8,196]{1,0:T(8,128)} %copy-done.36) | copy-start | bytes 18820
  1108.7 111.4 %copy-start.29 = (f32[8,196]{1,0:T(8,128)S(1)}, f32[8,196]{1,0:T(8,128)}, u32[]{:S(2)}) copy-start(f32[8,196]{1,0:T(8,128)} %copy-done.28) | copy-start | bytes 18820
  1108.7 178.2 %all-to-all-start = ((bf16[32,2,16384]{2,1,0:T(2,128)(2,1)}), bf16[32,2,16384]{2,1,0:T(2,128)(2,1)}, u32[]{:S(2)}, u32[]{:S(2)}) async-start(bf16[32,2,16384]{2,1,0:T(2,128)(2,1)} %reshape.321), calls=%async_computation.4 | async-start | bytes 4194304 | tf_op jit(solution)/shard_map/all_to_all | solution.py:259
  1215.4 8.5 copy-start.8
  1220.2 11.0 slice-start
  1223.9 7.2 slice-start.1
  1231.2 5.8 copy-start.60
  1231.2 5.8 copy-start.62
  1231.2 5.8 copy-start.72
  1231.3 5.8 copy-start.63
  1231.3 5.8 copy-start.44
  1231.3 5.8 copy-start.61
  1231.3 5.8 copy-start.65
  1231.3 5.8 copy-start.66
  1231.3 5.8 copy-start.27
  1231.3 5.8 copy-start.59
  1231.3 53.5 %copy-start.52 = (f32[2,512]{1,0:T(2,128)S(1)}, f32[2,512]{1,0:T(2,128)}, u32[]{:S(2)}) copy-start(f32[2,512]{1,0:T(2,128)} %param.45) | copy-start | bytes 12292
  1231.4 53.5 %copy-start.53 = (f32[2,512]{1,0:T(2,128)S(1)}, f32[2,512]{1,0:T(2,128)}, u32[]{:S(2)}) copy-start(f32[2,512]{1,0:T(2,128)} %param.44) | copy-start | bytes 12292
  1231.4 53.5 %copy-start.67 = (f32[2,512]{1,0:T(2,128)S(1)}, f32[2,512]{1,0:T(2,128)}, u32[]{:S(2)}) copy-start(f32[2,512]{1,0:T(2,128)} %param.55) | copy-start | bytes 12292
  1231.4 53.5 %copy-start.68 = (f32[2,512]{1,0:T(2,128)S(1)}, f32[2,512]{1,0:T(2,128)}, u32[]{:S(2)}) copy-start(f32[2,512]{1,0:T(2,128)} %param.54) | copy-start | bytes 12292
  1231.4 53.5 %copy-start.69 = (f32[2,512]{1,0:T(2,128)S(1)}, f32[2,512]{1,0:T(2,128)}, u32[]{:S(2)}) copy-start(f32[2,512]{1,0:T(2,128)} %param.53) | copy-start | bytes 12292
  1231.4 53.5 %copy-start.70 = (f32[2,512]{1,0:T(2,128)S(1)}, f32[2,512]{1,0:T(2,128)}, u32[]{:S(2)}) copy-start(f32[2,512]{1,0:T(2,128)} %param.52) | copy-start | bytes 12292
  1231.4 54.2 %copy-start.55 = (f32[169,16]{0,1:T(8,128)S(1)}, f32[169,16]{0,1:T(8,128)}, u32[]{:S(2)}) copy-start(f32[169,16]{0,1:T(8,128)} %param.47) | copy-start | bytes 32452
  1231.4 54.2 %copy-start.56 = (f32[169,16]{0,1:T(8,128)S(1)}, f32[169,16]{0,1:T(8,128)}, u32[]{:S(2)}) copy-start(f32[169,16]{0,1:T(8,128)} %param.59) | copy-start | bytes 32452
  1231.4 54.2 %copy-start.57 = (f32[169,16]{0,1:T(8,128)S(1)}, f32[169,16]{0,1:T(8,128)}, u32[]{:S(2)}) copy-start(f32[169,16]{0,1:T(8,128)} %param.58) | copy-start | bytes 32452
  1235.3 51.0 %copy-start.35 = (f32[4608]{0:T(1024)S(1)}, f32[4608]{0:T(1024)}, u32[]{:S(2)}) copy-start(f32[4608]{0:T(1024)} %param.46) | copy-start | bytes 55300
  1235.3 51.0 %copy-start.48 = (f32[4608]{0:T(1024)S(1)}, f32[4608]{0:T(1024)}, u32[]{:S(2)}) copy-start(f32[4608]{0:T(1024)} %param.57) | copy-start | bytes 55300
  1235.3 50.9 %copy-start.49 = (f32[4608]{0:T(1024)S(1)}, f32[4608]{0:T(1024)}, u32[]{:S(2)}) copy-start(f32[4608]{0:T(1024)} %param.56) | copy-start | bytes 55300
  1297.4 11.1 copy-start.6
  (27 other events, 83.8 us)
Sparse Core Ops, SparseCore 0:
  10.9 58.4 all-gather.7
  72.3 55.3 all-gather.9
  130.5 55.2 all-gather.11
  322.0 133.6 reduce-scatter.6
  462.4 97.4 reduce-scatter.4
  562.1 139.9 reduce-scatter.8
  704.5 136.9 reduce-scatter.10
  845.4 49.5 all-gather.15
  898.8 57.8 all-gather.13
  960.4 60.8 all-gather.17
  1025.2 60.5 all-gather.19
where the time goes:
time: 1330 us; the launch traced here: 1320 us
  waiting for transfers between devices  609 us (46%)
  matrix products  214 us (16%)
  local copies, waits for them, and re-layouts  135 us (10%)
  other arithmetic  120 us (9%)
  starting transfers between devices  108 us (8%)
  blocking collectives  94.6 us (7%)
  loops' own time  25.9 us (2%)
  between operations  16.6 us (1%)
    reduce_scatter x1, waiting for transfers between devices, local(): lax.psum_scatter(expand_term, 'dp', scatter_dimension=0, tiled=True)  141 us
    reduce_scatter x1, waiting for transfers between devices, local(): lax.psum_scatter(project_term, 'dp', scatter_dimension=0, tiled=True)  137 us
    all_gather x4, waiting for transfers between devices, local(): whole = lax.all_gather(momenta_next, 'dp', axis=0, tiled=True)  121 us
    all_to_all x1, starting transfers between devices, local(): lax.all_to_all(as_sent(packed), 'dp', split_axis=0, concat_axis=0, tiled=...  107 us
    reduce_scatter x1, waiting for transfers between devices, local(): lax.psum_scatter(attend_term, 'dp', scatter_dimension=0, tiled=True)  103 us
    reduce_scatter x1, waiting for transfers between devices, local(): lax.psum_scatter(merge_term, 'dp', scatter_dimension=0, tiled=True)  101 us
    all_gather x1, blocking collectives, local(): lax.all_gather(merge_weight, 'dp', axis=0, tiled=True)  47.8 us
    psum x1, blocking collectives, local(): lax.psum((jnp.stack([gain_one, gain_two]), jnp.stack([shift_one, shift_tw...  46.8 us
  transfers between devices with their start and end apart: 12, of which 8 were waited for; matrix products, arithmetic and copies ran while one was open for 21% of the time, Pallas kernels for 0%

commit v1 on v0

--- a/solution.py
+++ b/solution.py
@@ -122,9 +122,26 @@
     hidden_units = expand_weight.shape[1]
     scale = 1.0 / math.sqrt(width // HEADS)
     grad_scale = 1.0 / math.sqrt(slots * devices * PATCHES)
+
+    def joints_try_all(patch, row_axis="dp"):
+        w1, main, frame_out = (lax.axis_size(row_axis), lax.axis_index(row_axis), patch.shape[0])
+        far_arr, opened = (patch, 1)
+        while opened < w1:
+            far_arr = jnp.concatenate(
+                [
+                    far_arr,
+                    lax.ppermute(
+                        far_arr, row_axis, tuple(((c, (c - opened) % w1) for c in range(w1)))
+                    ),
+                ],
+                axis=0,
+            )
+            opened = 2 * opened
+        return jnp.roll(far_arr, main * frame_out, 0)
+
     gathered = (
         lax.all_gather(attend_weight, "dp", axis=0, tiled=True),
-        lax.all_gather(merge_weight, "dp", axis=0, tiled=True),
+        joints_try_all(merge_weight),
         lax.all_gather(expand_weight, "dp", axis=0, tiled=True),
         lax.all_gather(project_weight, "dp", axis=0, tiled=True),
     )

time: 1330 us -> 1360 us (1.023)
  local copies, waits for them, and re-layouts: 135 us -> 149 us
    unnamed x159 -> x169, local copies, waits for them, and re-layouts: 37 us -> 43.3 us
  transfers between devices with their start and end apart: 12 -> 17, of which waited for: 8 -> 10; matrix products, arithmetic and copies ran while one was open for 21% -> 21% of each run, Pallas kernels for 0% -> 0%
where the time goes in v1:
time: 1360 us; the launch traced here: 1350 us
  waiting for transfers between devices  609 us (45%)
  matrix products  214 us (16%)
  local copies, waits for them, and re-layouts  149 us (11%)
  other arithmetic  121 us (9%)
  starting transfers between devices  116 us (9%)
  blocking collectives  98.9 us (7%)
  loops' own time  25.9 us (2%)
  between operations  16.6 us (1%)
    reduce_scatter x1, waiting for transfers between devices, local(): lax.psum_scatter(expand_term, 'dp', scatter_dimension=0, tiled=True)  140 us
    reduce_scatter x1, waiting for transfers between devices, local(): lax.psum_scatter(project_term, 'dp', scatter_dimension=0, tiled=True)  137 us
    all_gather x4, waiting for transfers between devices, local(): whole = lax.all_gather(momenta_next, 'dp', axis=0, tiled=True)  121 us
    all_to_all x1, starting transfers between devices, local(): lax.all_to_all(as_sent(packed), 'dp', split_axis=0, concat_axis=0, tiled=...  107 us
    reduce_scatter x1, waiting for transfers between devices, local(): lax.psum_scatter(attend_term, 'dp', scatter_dimension=0, tiled=True)  103 us
    reduce_scatter x1, waiting for transfers between devices, local(): lax.psum_scatter(merge_term, 'dp', scatter_dimension=0, tiled=True)  98.1 us
    all_gather x1, blocking collectives, local(): lax.all_gather(merge_weight, 'dp', axis=0, tiled=True)  52.1 us
    psum x1, blocking collectives, local(): lax.psum((jnp.stack([gain_one, gain_two]), jnp.stack([shift_one, shift_tw...  46.8 us
  transfers between devices with their start and end apart: 17, of which 10 were waited for; matrix products, arithmetic and copies ran while one was open for 21% of the time, Pallas kernels for 0%

profile of v1, /device:TPU:0, one launch (start us, length us, event | category | flops | bytes accessed | tf_op | source)
XLA Modules:
  0.0 1350.9 jit_solution(10459665653057383691)
XLA Ops:
  8.7 6.4 collective-permute-start
  38.3 3.8 collective-permute-done.3
  46.6 3.8 reshape.277
  53.7 52.1 %all_gather.42 = bf16[512,512]{1,0:T(8,128)(2,1)} all-gather(bf16[16,512]{1,0:T(8,128)(2,1)S(1)} %copy-done.23), channel_id=1, replica_groups=mesh['dp'=32] {'dp'}, dimensions={0}, use_global_device_ids=true | all-gather | bytes 540672 | tf_op jit(solution)/shard_map/all_gather | solution.py:194
  110.4 6.5 fusion.126
  117.4 3.7 copy.261
  123.5 3.6 copy.260
  130.9 11.7 fusion.127
  142.6 7.6 fusion.76
  155.4 5.2 reshape.298
  160.5 4.5 copy.305
  172.2 9.4 fusion.68
  181.6 4.6 copy-done.10
  186.2 31.4 %multiply_convert_fusion.1 = (bf16[8,196,2048]{2,1,0:T(8,128)(2,1)}, f32[8,196,2048]{2,1,0:T(8,128)}) fusion(f32[8,196,2048]{2,1,0:T(8,128)S(1)} %get-tuple-element.278, f32[2048]{0:T(1024)S(1)} %copy-done.47, u8[196,2048]{1,0:T(8,128)(4,1)S(1)} %get-tuple-element.201, u8[196,2048]{1,0:T(8,128)(4,1)S(1)} %get-tuple-element.200), kind=kLoop, calls=%fused_computation.103 | loop fusion | flops 227999744 | bytes 32923648 | tf_op jit(solution)/shard_map/convert_element_type | solution.py:186
  217.6 18.7 %convert_reduce_fusion.1 = (f32[2048]{0:T(1024)}, bf16[8,196,2048]{2,1,0:T(8,128)(2,1)}) fusion(f32[8,196,2048]{2,1,0:T(8,128)} %get-tuple-element.249, bf16[2048,512]{1,0:T(8,128)(2,1)} %all-gather.12.cloned.1.call-done, f32[8]{0:T(128)} %compare_convert_fusion, bf16[8,196,512]{2,0,1:T(8,128)(2,1)} %param.35, f32[8,196,2048]{2,1,0:T(8,128)} %copy-done.10, ...), kind=kOutput, calls=%fused_computation.101 | convolution fusion | flops 3345332224 | bytes 35831840 | tf_op jit(solution)/shard_map/itd,fd->itf/dot_general | solution.py:201
  236.3 6.8 fusion.116
  254.5 3.8 reshape.299
  262.8 8.2 reshape.282
  270.9 10.5 copy.230
  281.4 13.1 multiply_reduce_fusion.4
  294.6 14.6 %convert_reduce_fusion = (f32[16,49,49]{1,2,0:T(8,128)}, bf16[32,16,49,49]{2,3,1,0:T(8,128)(2,1)}) fusion(f32[32,16,49,49]{2,3,1,0:T(8,128)} %get-tuple-element.281, f32[32,16,49]{2,1,0:T(8,128)S(1)} %get-tuple-element.280, f32[32,16,49,49]{2,3,1,0:T(8,128)} %get-tuple-element.277, f32[32,16,49]{2,1,0:T(8,128)S(1)} %get-tuple-element.276), kind=kLoop, calls=%fused_computation.90 | loop fusion | flops 7337456 | bytes 12647488 | tf_op jit(solution)/shard_map/reduce_sum | solution.py:221
  309.2 8.5 multiply_convert_fusion.2
  317.6 10.3 convolution_convert_fusion
  328.0 8.8 fusion.79
  339.1 4.9 copy.235
  344.0 4.9 copy.236
  348.9 4.9 copy.237
  353.8 4.9 convert_reduce_fusion.2
  361.1 5.2 fusion.69
  366.4 9.1 convolution_bitcast_fusion.2
  377.0 9.3 convolution_bitcast_fusion.1
  386.4 98.1 %reduce-scatter.7.cloned.1.call-done = f32[16,512]{1,0:T(8,128)} async-done(((f32[512,512]{1,0:T(8,128)}), f32[16,512]{1,0:T(8,128)}) %reduce-scatter.7.cloned.1.call-update) | async-done | bytes 32784 | tf_op jit(solution)/shard_map/reduce_scatter | solution.py:245
  486.0 102.8 %reduce-scatter.5.cloned.1.call-done = f32[16,1536]{1,0:T(8,128)} async-done(((f32[512,1536]{1,0:T(8,128)}), f32[16,1536]{1,0:T(8,128)}) %reduce-scatter.5.cloned.1.call-update) | async-done | bytes 98320 | tf_op jit(solution)/shard_map/reduce_scatter | solution.py:244
  590.4 140.5 %reduce-scatter.9.cloned.1.call-done = f32[16,2048]{1,0:T(8,128)} async-done(((f32[512,2048]{1,0:T(8,128)}), f32[16,2048]{1,0:T(8,128)}) %reduce-scatter.9.cloned.1.call-update) | async-done | bytes 131088 | tf_op jit(solution)/shard_map/reduce_scatter | solution.py:246
  733.1 137.0 %reduce-scatter.11.cloned.1.call-done = f32[64,512]{1,0:T(8,128)} async-done(((f32[2048,512]{1,0:T(8,128)}), f32[64,512]{1,0:T(8,128)}) %reduce-scatter.11.cloned.1.call-update) | async-done | bytes 131088 | tf_op jit(solution)/shard_map/reduce_scatter | solution.py:247
  872.5 7.0 fusion.51
  879.4 3.8 reshape.285
  892.2 31.3 %all-gather.16.cloned.1.call-done = f32[512,512]{1,0:T(8,128)} async-done(((f32[16,512]{1,0:T(8,128)}), f32[512,512]{1,0:T(8,128)}) %all-gather.16.cloned.1.call-update) | async-done | bytes 1048592 | tf_op jit(solution)/shard_map/all_gather | solution.py:262
  923.4 11.3 conditional.5
  934.7 50.5 %all-gather.14.cloned.1.call-done = f32[512,1536]{1,0:T(8,128)} async-done(((f32[16,1536]{1,0:T(8,128)}), f32[512,1536]{1,0:T(8,128)}) %all-gather.14.cloned.1.call-update) | async-done | bytes 3145744 | tf_op jit(solution)/shard_map/all_gather | solution.py:262
  985.2 77.7 %conditional.4 = (f32[32,32768]{1,0:T(8,128)}) conditional(s32[]{:T(128)} %convert_element_type.166, () %tuple.40, f32[512,1536]{1,0:T(8,128)} %all-gather.14.cloned.1.call-done), branch_computations={%region_12.13_spmd, %region_13.15_spmd} | conditional | flops 56387174400 | bytes 97517640 | solution.py:265
  989.2 8.3 fusion.5
  999.5 5.5 convolution_add_fusion.4
  1005.0 5.4 fusion.128
  1012.4 5.5 convolution_add_fusion.3
  1017.9 5.4 fusion.129
  1025.2 5.5 convolution_add_fusion.2
  1030.7 5.6 fusion.130
  1038.3 5.5 convolution_add_fusion.1
  1043.8 5.4 fusion.131
  1051.1 5.4 convolution_add_fusion
  1058.5 4.2 pad.16
  1062.9 12.3 conditional.6
  1075.2 39.0 %all-gather.20.cloned.1.call-done = f32[2048,512]{1,0:T(8,128)} async-done(((f32[64,512]{1,0:T(8,128)}), f32[2048,512]{1,0:T(8,128)}) %all-gather.20.cloned.1.call-update) | async-done | bytes 4194320 | tf_op jit(solution)/shard_map/all_gather | solution.py:262
  1114.3 8.3 conditional.7
  1122.5 6.6 fusion.84
  1132.6 4.6 reshape.322
  1137.2 106.8 %all-to-all-start = ((bf16[32,2,16384]{2,1,0:T(2,128)(2,1)}), bf16[32,2,16384]{2,1,0:T(2,128)(2,1)}, u32[]{:S(2)}, u32[]{:S(2)}) async-start(bf16[32,2,16384]{2,1,0:T(2,128)(2,1)} %reshape.322), calls=%async_computation.4 | async-start | bytes 4194304 | tf_op jit(solution)/shard_map/all_to_all | solution.py:276
  1244.0 4.7 fusion.65
  1248.8 3.7 fusion.63
  1260.0 3.8 multiply_convert_fusion.3
  1266.6 46.8 %all-reduce.4 = (f32[2,512]{1,0:T(2,128)S(1)}, f32[2,512]{1,0:T(2,128)S(1)}, f32[4608]{0:T(1024)S(1)}, f32[169,16]{0,1:T(8,128)S(1)}) all-reduce(f32[2,512]{1,0:T(2,128)S(1)} %pad_maximum_fusion.12, f32[2,512]{1,0:T(2,128)S(1)} %pad_maximum_fusion.13, f32[4608]{0:T(1024)S(1)} %pad_maximum_fusion.11, ...), channel_id=1, replica_groups=mesh['dp'=32] {'dp'}, use_global_device_ids=true, to_apply=%region_29.30 | all-reduce | flops 9360 | bytes 74880 | tf_op jit(solution)/shard_map/psum | solution.py:249
  1315.5 10.4 reshape.323
  1325.9 11.1 convert_element_type.171
  (303 shorter events, 137.3 us)
Async XLA Ops:
  7.2 15.4 %copy-start.2 = (bf16[8,196,512]{2,0,1:T(8,128)(2,1)S(1)}, bf16[8,196,512]{2,0,1:T(8,128)(2,1)}, u32[]{:S(2)}) copy-start(bf16[8,196,512]{2,0,1:T(8,128)(2,1)} %param.34) | copy-start | bytes 4816900
  7.2 103.2 %all-gather.8.cloned.1.call-start = ((), (), s32[]{:S(2)}) async-start(), calls=%async_computation.5 | async-start | bytes 1622016 | tf_op jit(solution)/shard_map/all_gather | solution.py:143
  7.9 164.2 %all-gather.10.cloned.1.call-start = ((), (), s32[]{:S(2)}) async-start(), calls=%async_computation.6 | async-start | bytes 2162688 | tf_op jit(solution)/shard_map/all_gather | solution.py:145
  8.7 208.8 %all-gather.12.cloned.1.call-start = ((), (), s32[]{:S(2)}) async-start(), calls=%async_computation.7 | async-start | bytes 2162688 | tf_op jit(solution)/shard_map/all_gather | solution.py:146
  8.7 19.4 %collective-permute-start = (bf16[16,512]{1,0:T(8,128)(2,1)}, bf16[16,512]{1,0:T(8,128)(2,1)S(1)}, u32[]{:S(2)}, u32[]{:S(2)}) collective-permute-start(bf16[16,512]{1,0:T(8,128)(2,1)} %param.41), channel_id=1, source_target_pairs={{0,31},{1,0},{2,1},{3,2},{4,3},{5,4},{6,5},{7,6},{8,7},{9,8},{10,9... | collective-permute-start | bytes 49160 | tf_op jit(solution)/shard_map/ppermute | solution.py:133
  15.2 469.3 %reduce-scatter.7.cloned.1.call-start = ((), (), s32[]{:S(2)}) async-start(), calls=%async_computation.10 | async-start | bytes 1081344 | tf_op jit(solution)/shard_map/reduce_scatter | solution.py:245
  17.6 6.9 copy-start.25
  28.2 4.0 collective-permute-start.1
  32.2 4.3 collective-permute-start.2
  36.5 5.6 collective-permute-start.3
  42.8 63.1 %collective-permute-start.4 = (bf16[256,512]{1,0:T(8,128)(2,1)}, bf16[256,512]{1,0:T(8,128)(2,1)S(1)}, u32[]{:S(2)}, u32[]{:S(2)}) collective-permute-start(bf16[256,512]{1,0:T(8,128)(2,1)} %get-tuple-element.258), channel_id=1, source_target_pairs={{0,16},{1,17},{2,18},{3,19},{4,20},{5,21},{6,22},{7,23},{8,24},{9,... | collective-permute-start | bytes 786440 | tf_op jit(solution)/shard_map/ppermute | solution.py:133
  46.6 63.8 %slice-start.2 = ((f32[4608]{0:T(1024)}), f32[1536]{0:T(1024)S(1)}, s32[]{:S(2)}) async-start(f32[4608]{0:T(1024)} %param.46), calls=%async_computation.18 | async-start | bytes 16384 | tf_op jit(solution)/shard_map/slice | solution.py:159
  50.4 66.5 %copy-start.18 = (bf16[32,49,512]{2,0,1:T(8,128)(2,1)}, bf16[32,49,512]{2,0,1:T(8,128)(2,1)S(1)}, u32[]{:S(2)}) copy-start(bf16[32,49,512]{2,0,1:T(8,128)(2,1)S(1)} %reshape.277) | copy-start | bytes 4816900
  142.6 9.6 copy-start.27
  142.6 9.6 copy-start.64
  170.5 195.9 %copy-start = (f32[8,196,512]{2,1,0:T(8,128)}, f32[8,196,512]{2,1,0:T(8,128)S(1)}, u32[]{:S(2)}) copy-start(f32[8,196,512]{2,1,0:T(8,128)S(1)} %get-tuple-element.251) | copy-start | bytes 9633796
  172.2 14.0 %copy-start.47 = (f32[2048]{0:T(1024)S(1)}, f32[2048]{0:T(1024)}, u32[]{:S(2)}) copy-start(f32[2048]{0:T(1024)} %slice.126) | copy-start | bytes 24580
  217.5 18.7 %copy-start.43 = (f32[1,512]{1,0:T(1,128)S(1)}, f32[1,512]{1,0:T(1,128)}, u32[]{:S(2)}) copy-start(f32[1,512]{1,0:T(1,128)} %get-tuple-element.270) | copy-start | bytes 6148
  217.5 18.7 %copy-start.77 = (bf16[512,2048]{1,0:T(8,128)(2,1)S(1)}, bf16[512,2048]{1,0:T(8,128)(2,1)}, u32[]{:S(2)}) copy-start(bf16[512,2048]{1,0:T(8,128)(2,1)} %all-gather.10.cloned.1.call-done) | copy-start | bytes 6291460
  236.3 6.8 copy-start.40
  317.6 10.3 copy-start.15
  328.0 8.8 copy-start.13
  328.0 8.8 copy-start.17
  353.8 235.0 %reduce-scatter.5.cloned.1.call-start = ((), (), s32[]{:S(2)}) async-start(), calls=%async_computation.8 | async-start | bytes 3244032 | tf_op jit(solution)/shard_map/reduce_scatter | solution.py:244
  353.8 7.3 copy-start.19
  366.4 364.5 %reduce-scatter.9.cloned.1.call-start = ((), (), s32[]{:S(2)}) async-start(), calls=%async_computation.12 | async-start | bytes 4325376 | tf_op jit(solution)/shard_map/reduce_scatter | solution.py:246
  375.6 494.5 %reduce-scatter.11.cloned.1.call-start = ((), (), s32[]{:S(2)}) async-start(), calls=%async_computation.14 | async-start | bytes 4325376 | tf_op jit(solution)/shard_map/reduce_scatter | solution.py:247
  386.3 98.2 %copy-start.46 = (f32[16,512]{1,0:T(8,128)S(1)}, f32[16,512]{1,0:T(8,128)}, u32[]{:S(2)}) copy-start(f32[16,512]{1,0:T(8,128)} %param.49) | copy-start | bytes 98308
  386.3 202.5 %copy-start.34 = (f32[16,1536]{1,0:T(8,128)S(1)}, f32[16,1536]{1,0:T(8,128)}, u32[]{:S(2)}) copy-start(f32[16,1536]{1,0:T(8,128)} %param.48) | copy-start | bytes 294916
  386.3 344.6 %copy-start.31 = (f32[16,2048]{1,0:T(8,128)S(1)}, f32[16,2048]{1,0:T(8,128)}, u32[]{:S(2)}) copy-start(f32[16,2048]{1,0:T(8,128)} %param.50) | copy-start | bytes 393220
  386.3 483.7 %copy-start.32 = (f32[64,512]{1,0:T(8,128)S(1)}, f32[64,512]{1,0:T(8,128)}, u32[]{:S(2)}) copy-start(f32[64,512]{1,0:T(8,128)} %param.51) | copy-start | bytes 393220
  386.3 486.1 %copy-start.78 = (bf16[512,1536]{1,0:T(8,128)(2,1)S(1)}, bf16[512,1536]{1,0:T(8,128)(2,1)}, u32[]{:S(2)}) copy-start(bf16[512,1536]{1,0:T(8,128)(2,1)} %all-gather.8.cloned.1.call-done) | copy-start | bytes 4718596
  386.4 537.1 %all-gather.16.cloned.1.call-start = ((), (), s32[]{:S(2)}) async-start(), calls=%async_computation.11 | async-start | bytes 1081344 | tf_op jit(solution)/shard_map/all_gather | solution.py:262
  485.9 499.3 %all-gather.14.cloned.1.call-start = ((), (), s32[]{:S(2)}) async-start(), calls=%async_computation.9 | async-start | bytes 3244032 | tf_op jit(solution)/shard_map/all_gather | solution.py:262
  590.4 472.5 %all-gather.18.cloned.1.call-start = ((), (), s32[]{:S(2)}) async-start(), calls=%async_computation.13 | async-start | bytes 4325376 | tf_op jit(solution)/shard_map/all_gather | solution.py:262
  732.6 381.7 %all-gather.20.cloned.1.call-start = ((), (), s32[]{:S(2)}) async-start(), calls=%async_computation.15 | async-start | bytes 4325376 | tf_op jit(solution)/shard_map/all_gather | solution.py:262
  989.2 10.2 copy-start.16
  1132.6 111.4 %copy-start.4 = (bf16[8,196,512]{2,0,1:T(8,128)(2,1)S(1)}, bf16[8,196,512]{2,0,1:T(8,128)(2,1)}, u32[]{:S(2)}) copy-start(bf16[8,196,512]{2,0,1:T(8,128)(2,1)} %param.34) | copy-start | bytes 4816900
  1132.6 111.4 %copy-start.26 = (f32[8,196]{1,0:T(8,128)S(1)}, f32[8,196]{1,0:T(8,128)}, u32[]{:S(2)}) copy-start(f32[8,196]{1,0:T(8,128)} %copy-done.25) | copy-start | bytes 18820
  1132.6 111.4 %copy-start.42 = (f32[1,512]{1,0:T(1,128)S(1)}, f32[1,512]{1,0:T(1,128)}, u32[]{:S(2)}) copy-start(f32[1,512]{1,0:T(1,128)} %copy-done.41) | copy-start | bytes 6148
  1137.2 111.5 %copy-start.38 = (f32[8,196]{1,0:T(8,128)S(1)}, f32[8,196]{1,0:T(8,128)}, u32[]{:S(2)}) copy-start(f32[8,196]{1,0:T(8,128)} %copy-done.37) | copy-start | bytes 18820
  1137.2 111.6 %copy-start.30 = (f32[8,196]{1,0:T(8,128)S(1)}, f32[8,196]{1,0:T(8,128)}, u32[]{:S(2)}) copy-start(f32[8,196]{1,0:T(8,128)} %copy-done.29) | copy-start | bytes 18820
  1137.2 178.3 %all-to-all-start = ((bf16[32,2,16384]{2,1,0:T(2,128)(2,1)}), bf16[32,2,16384]{2,1,0:T(2,128)(2,1)}, u32[]{:S(2)}, u32[]{:S(2)}) async-start(bf16[32,2,16384]{2,1,0:T(2,128)(2,1)} %reshape.322), calls=%async_computation.4 | async-start | bytes 4194304 | tf_op jit(solution)/shard_map/all_to_all | solution.py:276
  1244.0 8.5 copy-start.8
  1248.8 11.0 slice-start
  1252.5 7.2 slice-start.1
  1259.9 5.8 copy-start.45
  1259.9 5.8 copy-start.61
  1259.9 5.8 copy-start.65
  1259.9 5.8 copy-start.28
  1259.9 5.8 copy-start.59
  1259.9 53.5 %copy-start.52 = (f32[2,512]{1,0:T(2,128)S(1)}, f32[2,512]{1,0:T(2,128)}, u32[]{:S(2)}) copy-start(f32[2,512]{1,0:T(2,128)} %param.45) | copy-start | bytes 12292
  1259.9 53.5 %copy-start.53 = (f32[2,512]{1,0:T(2,128)S(1)}, f32[2,512]{1,0:T(2,128)}, u32[]{:S(2)}) copy-start(f32[2,512]{1,0:T(2,128)} %param.44) | copy-start | bytes 12292
  1260.0 53.5 %copy-start.67 = (f32[2,512]{1,0:T(2,128)S(1)}, f32[2,512]{1,0:T(2,128)}, u32[]{:S(2)}) copy-start(f32[2,512]{1,0:T(2,128)} %param.55) | copy-start | bytes 12292
  1260.0 53.5 %copy-start.68 = (f32[2,512]{1,0:T(2,128)S(1)}, f32[2,512]{1,0:T(2,128)}, u32[]{:S(2)}) copy-start(f32[2,512]{1,0:T(2,128)} %param.54) | copy-start | bytes 12292
  1260.0 53.5 %copy-start.69 = (f32[2,512]{1,0:T(2,128)S(1)}, f32[2,512]{1,0:T(2,128)}, u32[]{:S(2)}) copy-start(f32[2,512]{1,0:T(2,128)} %param.53) | copy-start | bytes 12292
  1260.0 53.5 %copy-start.70 = (f32[2,512]{1,0:T(2,128)S(1)}, f32[2,512]{1,0:T(2,128)}, u32[]{:S(2)}) copy-start(f32[2,512]{1,0:T(2,128)} %param.52) | copy-start | bytes 12292
  1260.0 54.2 %copy-start.55 = (f32[169,16]{0,1:T(8,128)S(1)}, f32[169,16]{0,1:T(8,128)}, u32[]{:S(2)}) copy-start(f32[169,16]{0,1:T(8,128)} %param.47) | copy-start | bytes 32452
  1260.0 54.2 %copy-start.56 = (f32[169,16]{0,1:T(8,128)S(1)}, f32[169,16]{0,1:T(8,128)}, u32[]{:S(2)}) copy-start(f32[169,16]{0,1:T(8,128)} %param.59) | copy-start | bytes 32452
  1260.0 54.2 %copy-start.57 = (f32[169,16]{0,1:T(8,128)S(1)}, f32[169,16]{0,1:T(8,128)}, u32[]{:S(2)}) copy-start(f32[169,16]{0,1:T(8,128)} %param.58) | copy-start | bytes 32452
  1263.9 51.0 %copy-start.36 = (f32[4608]{0:T(1024)S(1)}, f32[4608]{0:T(1024)}, u32[]{:S(2)}) copy-start(f32[4608]{0:T(1024)} %param.46) | copy-start | bytes 55300
  1263.9 51.0 %copy-start.49 = (f32[4608]{0:T(1024)S(1)}, f32[4608]{0:T(1024)}, u32[]{:S(2)}) copy-start(f32[4608]{0:T(1024)} %param.57) | copy-start | bytes 55300
  1263.9 50.9 %copy-start.50 = (f32[4608]{0:T(1024)S(1)}, f32[4608]{0:T(1024)}, u32[]{:S(2)}) copy-start(f32[4608]{0:T(1024)} %param.56) | copy-start | bytes 55300
  1325.9 11.1 copy-start.6
  (32 other events, 111.4 us)
Sparse Core Ops, SparseCore 0:
  10.9 60.1 all-gather.7
  74.0 55.5 all-gather.9
  132.4 55.2 all-gather.11
  353.9 130.6 reduce-scatter.6
  491.3 97.4 reduce-scatter.4
  591.0 139.8 reduce-scatter.8
  733.3 136.7 reduce-scatter.10
  873.9 49.5 all-gather.15
  927.3 57.8 all-gather.13
  988.9 60.8 all-gather.17
  1053.6 60.5 all-gather.19
